TPU v7x, 32 devices: a whole 2x2x4 slice. The times are simulated.
32 devices in a mesh: dp: 16 (over z, y, core), tensor: 2 (over x).
Axes of the slice: x: 2, y: 2, z: 4, core: 2. Of those that a mesh axis runs over, the one named last changes fastest.
Arguments:
- tokens: bfloat16 [32768, 1024], P(('dp', 'tensor')), may hold values from -6 to 6
- gain_one: float32 [1024], replicated, may hold values from 0.5 to 1.5
- gain_two: float32 [1024], replicated, may hold values from 0.5 to 1.5
- w_query: bfloat16 [1024, 1024], P(None, 'tensor'), may hold values from -0.1875 to 0.1875
- w_key: bfloat16 [512, 1024], P('tensor'), may hold values from -0.1875 to 0.1875
- w_value: bfloat16 [512, 1024], P('tensor'), may hold values from -0.1875 to 0.1875
- w_out: bfloat16 [1024, 1024], P('tensor'), may hold values from -1 to 1
- w_gate: bfloat16 [32, 512, 1024], P(None, 'tensor'), may hold values from -0.1875 to 0.1875
- w_up: bfloat16 [32, 512, 1024], P(None, 'tensor'), may hold values from -0.1875 to 0.1875
- w_down: bfloat16 [32, 512, 1024], P(None, 'tensor'), may hold values from -1 to 1
- slot_index: int32 [16, 32, 640], P('dp'), may hold values from 0 to 2047, as said below
- slot_gate: float32 [16, 32, 640], P('dp'), may hold values from 0 to 0.19, as said below
- grad_output: bfloat16 [32768, 1024], P(('dp', 'tensor')), may hold values from -6 to 6
Outputs:
- output: bfloat16 [32768, 1024], P(('dp', 'tensor'))
- grad_tokens: bfloat16 [32768, 1024], P('dp')
- grad_gain_one: float32 [1024], replicated
- grad_gain_two: float32 [1024], replicated
- grad_w_query: float32 [1024, 1024], P(None, 'tensor')
- grad_w_key: float32 [512, 1024], P('tensor')
- grad_w_value: float32 [512, 1024], P('tensor')
- grad_w_out: float32 [1024, 1024], P('tensor')
- grad_w_gate: float32 [32, 512, 1024], P(None, 'tensor')
- grad_w_up: float32 [32, 512, 1024], P(None, 'tensor')
- grad_w_down: float32 [32, 512, 1024], P(None, 'tensor')
Inputs may be any that keep to these rules, and one draw needn't show every extreme that they name: `slot_index`: in each sequence group the 640 slots of one expert name distinct tokens of that group. `slot_gate`: in each expert's block the live slots (gate above zero) come first, followed by empty slots of gate zero; a block has 320 to 640 live slots, and in every sequence group some block is full.
All inputs are finite; a program needn't handle non-finite values.
Results may differ from a plain program's by a relative error of at most 0.023.
Values may be sent and summed in bfloat16 or wider, within the bound.
No kernel may reach another device: no remote copies, remote signals or barrier semaphores. Data moves between devices by JAX's collectives and lax.ppermute only.
A program may use at most 448 MiB of HBM per device.

v0:
```python
import math
import jax
import jax.numpy as jnp
from jax import lax
from jax.sharding import PartitionSpec as P

HD = 64
SEQ_LEN = 1024
EPS = 1e-05
THETA = 10000.0
MASKED = -1e30


def rope_tables(row_count, head_size):
    position = (jnp.arange(row_count) % SEQ_LEN).astype(jnp.float32)
    exponent = jnp.arange(head_size // 2).astype(jnp.float32) * (2.0 / head_size)
    angles = position[:, None] * jnp.power(THETA, -exponent)[None, :]
    return (jnp.cos(angles)[:, None, :], jnp.sin(angles)[:, None, :])


def rotate(values, cosine, sine_tab):
    half_size = values.shape[-1] // 2
    first, second = (values[..., :half_size], values[..., half_size:])
    return jnp.concatenate(
        [first * cosine - second * sine_tab, second * cosine + first * sine_tab], axis=-1
    )


def unrotate(grads_in, cosine, sine_tab):
    half_size = grads_in.shape[-1] // 2
    first, second = (grads_in[..., :half_size], grads_in[..., half_size:])
    return jnp.concatenate(
        [first * cosine + second * sine_tab, second * cosine - first * sine_tab], axis=-1
    )


def normalize(values, gain):
    inverse = lax.rsqrt(jnp.mean(values * values, axis=-1, keepdims=True) + EPS)
    return (values * inverse * gain, inverse)


def norm_back(values, inverse, gain, grad_normed):
    scaled = grad_normed * gain
    return inverse * scaled - values * inverse**3 * jnp.mean(
        scaled * values, axis=-1, keepdims=True
    )


def causal_mask(length):
    query_pos = lax.broadcasted_iota(jnp.int32, (length, length), 0)
    key_pos = lax.broadcasted_iota(jnp.int32, (length, length), 1)
    return key_pos <= query_pos


def attend_forward(members):
    queries, keys, values = members
    score_scale = queries.shape[-1] ** (-0.5)
    scores = (
        jnp.einsum("qgrd,kgd->grqk", queries, keys, preferred_element_type=jnp.float32)
        * score_scale
    )
    scores = jnp.where(causal_mask(queries.shape[0]), scores, MASKED)
    row_peak = jnp.max(scores, axis=-1, keepdims=True)
    exponent = jnp.exp(scores - row_peak)
    row_total = jnp.sum(exponent, axis=-1, keepdims=True)
    weights = (exponent / row_total).astype(jnp.bfloat16)
    mixed = jnp.einsum(
        "grqk,kgd->qgrd", weights, values, preferred_element_type=jnp.float32
    ).astype(jnp.bfloat16)
    return (mixed, row_peak[..., 0] + jnp.log(row_total[..., 0]))


def attend_backward(members):
    queries, keys, values, grad_mixed, log_total = members
    score_scale = queries.shape[-1] ** (-0.5)
    scores = (
        jnp.einsum("qgrd,kgd->grqk", queries, keys, preferred_element_type=jnp.float32)
        * score_scale
    )
    scores = jnp.where(causal_mask(queries.shape[0]), scores, MASKED)
    weights = jnp.exp(scores - log_total[..., None])
    grad_weights = jnp.einsum(
        "qgrd,kgd->grqk", grad_mixed, values, preferred_element_type=jnp.float32
    )
    grad_values = jnp.einsum(
        "grqk,qgrd->kgd",
        weights.astype(jnp.bfloat16),
        grad_mixed,
        preferred_element_type=jnp.float32,
    )
    row_delta = jnp.sum(grad_weights * weights, axis=-1, keepdims=True)
    grad_scores = (weights * (grad_weights - row_delta)).astype(jnp.bfloat16)
    grad_queries = (
        jnp.einsum("grqk,kgd->qgrd", grad_scores, keys, preferred_element_type=jnp.float32)
        * score_scale
    )
    grad_keys = (
        jnp.einsum("grqk,qgrd->kgd", grad_scores, queries, preferred_element_type=jnp.float32)
        * score_scale
    )
    return (grad_queries, grad_keys, grad_values)


def per_device(
    tokens,
    gain_one,
    gain_two,
    w_query,
    w_key,
    w_value,
    w_out,
    w_gate,
    w_up,
    w_down,
    slot_index,
    slot_gate,
    grad_output,
):
    n_tensor = lax.axis_size("tensor")
    shard_rows, width = tokens.shape
    head_size = HD
    local_heads = w_query.shape[1] // head_size
    local_groups = w_key.shape[0] // head_size
    expert_count, hidden_local, _ = w_gate.shape
    sweeps = math.gcd(expert_count, 4)
    slot_rows = slot_index[0].reshape(sweeps, expert_count // sweeps, -1)
    slot_weight = slot_gate[0].reshape(sweeps, expert_count // sweeps, -1)
    gate_blocks = w_gate.reshape(sweeps, expert_count // sweeps, hidden_local, width)
    up_blocks = w_up.reshape(sweeps, expert_count // sweeps, hidden_local, width)
    down_blocks = w_down.reshape(sweeps, expert_count // sweeps, hidden_local, width)
    row_start = lax.axis_index("tensor") * shard_rows
    full_rows = lax.all_gather(tokens, "tensor", axis=0, tiled=True)
    row_count = full_rows.shape[0]
    seq_count = row_count // SEQ_LEN
    cosine, sine_tab = rope_tables(row_count, head_size)
    rows_float = full_rows.astype(jnp.float32)
    normed_one, inverse_one = normalize(rows_float, gain_one)
    normed_one = normed_one.astype(jnp.bfloat16)
    query_pre = jnp.dot(normed_one, w_query, preferred_element_type=jnp.float32)
    key_pre = jnp.einsum("td,kd->tk", normed_one, w_key, preferred_element_type=jnp.float32)
    values = jnp.einsum(
        "td,kd->tk", normed_one, w_value, preferred_element_type=jnp.float32
    ).astype(jnp.bfloat16)
    queries = rotate(query_pre.reshape(row_count, local_heads, head_size), cosine, sine_tab).astype(
        jnp.bfloat16
    )
    keys = rotate(key_pre.reshape(row_count, local_groups, head_size), cosine, sine_tab).astype(
        jnp.bfloat16
    )
    seq_queries = queries.reshape(
        seq_count, SEQ_LEN, local_groups, local_heads // local_groups, head_size
    )
    seq_keys = keys.reshape(seq_count, SEQ_LEN, local_groups, head_size)
    seq_values = values.reshape(seq_count, SEQ_LEN, local_groups, head_size)
    mixed, log_total = lax.map(attend_forward, (seq_queries, seq_keys, seq_values))
    mixed = mixed.reshape(row_count, local_heads * head_size)
    attn_part = jnp.dot(mixed, w_out, preferred_element_type=jnp.float32)
    attn_shard = lax.psum_scatter(attn_part, "tensor", scatter_dimension=0, tiled=True)
    residual = tokens.astype(jnp.float32) + attn_shard
    normed_shard, inverse_two = normalize(residual, gain_two)
    normed_two = lax.all_gather(normed_shard.astype(jnp.bfloat16), "tensor", axis=0, tiled=True)

    def expert_forward(running, members):
        slot_part, weight_part, gate_part, up_part, down_part = members
        gathered = normed_two[slot_part]
        gate_pre = jnp.einsum(
            "ecd,efd->ecf", gathered, gate_part, preferred_element_type=jnp.float32
        )
        up_pre = jnp.einsum("ecd,efd->ecf", gathered, up_part, preferred_element_type=jnp.float32)
        active = (jax.nn.silu(gate_pre) * up_pre).astype(jnp.bfloat16)
        expert_out = (
            jnp.einsum("ecf,efd->ecd", active, down_part, preferred_element_type=jnp.float32)
            * weight_part[..., None]
        )
        running = running.at[slot_part.reshape(-1)].add(expert_out.reshape(-1, width))
        return (running, ())

    mixture_part, saved = lax.scan(
        expert_forward,
        jnp.zeros((row_count, width), jnp.float32),
        (slot_rows, slot_weight, gate_blocks, up_blocks, down_blocks),
    )
    mixture = lax.psum_scatter(
        mixture_part.astype(jnp.bfloat16), "tensor", scatter_dimension=0, tiled=True
    ).astype(jnp.float32)
    output = (residual + mixture).astype(jnp.bfloat16)
    grad_full = lax.all_gather(grad_output, "tensor", axis=0, tiled=True)

    def expert_backward(running, members):
        slot_part, weight_part, gate_part, up_part, down_part, kept_part = members
        gathered = normed_two[slot_part]
        gate_pre = jnp.einsum(
            "ecd,efd->ecf", gathered, gate_part, preferred_element_type=jnp.float32
        )
        up_pre = jnp.einsum("ecd,efd->ecf", gathered, up_part, preferred_element_type=jnp.float32)
        sigmoid_val = jax.nn.sigmoid(gate_pre)
        silu_val = gate_pre * sigmoid_val
        active = (silu_val * up_pre).astype(jnp.bfloat16)
        grad_out = (grad_full[slot_part].astype(jnp.float32) * weight_part[..., None]).astype(
            jnp.bfloat16
        )
        grad_act = jnp.einsum(
            "ecd,efd->ecf", grad_out, down_part, preferred_element_type=jnp.float32
        )
        grad_gate = (
            grad_act * up_pre * sigmoid_val * (1.0 + gate_pre * (1.0 - sigmoid_val))
        ).astype(jnp.bfloat16)
        grad_up = (grad_act * silu_val).astype(jnp.bfloat16)
        grad_down_w = jnp.einsum(
            "ecf,ecd->efd", active, grad_out, preferred_element_type=jnp.float32
        )
        grad_gate_w = jnp.einsum(
            "ecf,ecd->efd", grad_gate, gathered, preferred_element_type=jnp.float32
        )
        grad_up_w = jnp.einsum(
            "ecf,ecd->efd", grad_up, gathered, preferred_element_type=jnp.float32
        )
        grad_gathered = jnp.einsum(
            "ecf,efd->ecd", grad_gate, gate_part, preferred_element_type=jnp.float32
        )
        grad_gathered = grad_gathered + jnp.einsum(
            "ecf,efd->ecd", grad_up, up_part, preferred_element_type=jnp.float32
        )
        running = running.at[slot_part.reshape(-1)].add(grad_gathered.reshape(-1, width))
        grad_triple = (grad_gate_w, grad_up_w, grad_down_w)
        return (running, grad_triple)

    grad_normed_part, expert_grads = lax.scan(
        expert_backward,
        jnp.zeros((row_count, width), jnp.float32),
        (slot_rows, slot_weight, gate_blocks, up_blocks, down_blocks, saved),
    )
    grad_w_gate = expert_grads[0].reshape(expert_count, hidden_local, width)
    grad_w_up = expert_grads[1].reshape(expert_count, hidden_local, width)
    grad_w_down = expert_grads[2].reshape(expert_count, hidden_local, width)
    shared = (
        lax.psum_scatter(
            grad_w_gate.astype(jnp.bfloat16), "dp", scatter_dimension=2, tiled=True
        ).astype(jnp.float32),
        lax.psum_scatter(
            grad_w_up.astype(jnp.bfloat16), "dp", scatter_dimension=2, tiled=True
        ).astype(jnp.float32),
        lax.psum_scatter(
            grad_w_down.astype(jnp.bfloat16), "dp", scatter_dimension=2, tiled=True
        ).astype(jnp.float32),
    )
    grad_w_gate, grad_w_up, grad_w_down = (
        lax.all_gather(shared[0].astype(jnp.bfloat16), "dp", axis=2, tiled=True).astype(
            jnp.float32
        ),
        lax.all_gather(shared[1].astype(jnp.bfloat16), "dp", axis=2, tiled=True).astype(
            jnp.float32
        ),
        lax.all_gather(shared[2].astype(jnp.bfloat16), "dp", axis=2, tiled=True).astype(
            jnp.float32
        ),
    )
    grad_normed_two = lax.psum_scatter(
        grad_normed_part.astype(jnp.bfloat16), "tensor", scatter_dimension=0, tiled=True
    ).astype(jnp.float32)
    gain_two_part = jnp.sum(grad_normed_two * residual * inverse_two, axis=0)
    grad_resid = grad_output.astype(jnp.float32) + norm_back(
        residual, inverse_two, gain_two, grad_normed_two
    )
    grad_attn = lax.all_gather(grad_resid.astype(jnp.bfloat16), "tensor", axis=0, tiled=True)
    grad_w_out = jnp.dot(mixed.T, grad_attn, preferred_element_type=jnp.float32)
    grad_mixed = jnp.dot(grad_attn, w_out.T, preferred_element_type=jnp.float32).astype(
        jnp.bfloat16
    )
    grad_mixed = grad_mixed.reshape(
        seq_count, SEQ_LEN, local_groups, local_heads // local_groups, head_size
    )
    grad_q_rot, grad_k_rot, grad_v_seq = lax.map(
        attend_backward, (seq_queries, seq_keys, seq_values, grad_mixed, log_total)
    )
    grad_q = unrotate(grad_q_rot.reshape(row_count, local_heads, head_size), cosine, sine_tab)
    grad_q = grad_q.reshape(row_count, local_heads * head_size).astype(jnp.bfloat16)
    grad_k = unrotate(grad_k_rot.reshape(row_count, local_groups, head_size), cosine, sine_tab)
    grad_k = grad_k.reshape(row_count, local_groups * head_size).astype(jnp.bfloat16)
    grad_v = grad_v_seq.reshape(row_count, local_groups * head_size).astype(jnp.bfloat16)
    grad_w_query = jnp.dot(normed_one.T, grad_q, preferred_element_type=jnp.float32)
    grad_w_key = jnp.dot(grad_k.T, normed_one, preferred_element_type=jnp.float32)
    grad_w_value = jnp.dot(grad_v.T, normed_one, preferred_element_type=jnp.float32)
    grad_normed_one = jnp.dot(grad_q, w_query.T, preferred_element_type=jnp.float32)
    grad_normed_one = grad_normed_one + jnp.dot(grad_k, w_key, preferred_element_type=jnp.float32)
    grad_normed_one = grad_normed_one + jnp.dot(grad_v, w_value, preferred_element_type=jnp.float32)
    gain_one_part = jnp.sum(grad_normed_one * rows_float * inverse_one, axis=0)
    gains_tile = jnp.broadcast_to(
        jnp.stack([gain_one_part, gain_two_part])[None], (n_tensor, 2, width)
    )
    grad_normed_shard, gains_sum = (
        lax.psum_scatter(
            grad_normed_one.astype(jnp.bfloat16), "tensor", scatter_dimension=0, tiled=True
        ).astype(jnp.float32),
        lax.psum_scatter(
            gains_tile.astype(jnp.bfloat16), "tensor", scatter_dimension=0, tiled=True
        ).astype(jnp.float32),
    )
    inverse_shard = lax.dynamic_slice_in_dim(inverse_one, row_start, shard_rows, 0)
    grad_input = grad_resid + norm_back(
        tokens.astype(jnp.float32), inverse_shard, gain_one, grad_normed_shard
    )
    grad_tokens = lax.all_gather(grad_input.astype(jnp.bfloat16), "tensor", axis=0, tiled=True)
    grad_w_query, grad_w_key, grad_w_value, grad_w_out, gains_total = (
        lax.psum(grad_w_query.astype(jnp.bfloat16), "dp").astype(jnp.float32),
        lax.psum(grad_w_key.astype(jnp.bfloat16), "dp").astype(jnp.float32),
        lax.psum(grad_w_value.astype(jnp.bfloat16), "dp").astype(jnp.float32),
        lax.psum(grad_w_out.astype(jnp.bfloat16), "dp").astype(jnp.float32),
        lax.psum(gains_sum.astype(jnp.bfloat16), "dp").astype(jnp.float32),
    )
    return (
        output,
        grad_tokens,
        gains_total[0, 0],
        gains_total[0, 1],
        grad_w_query,
        grad_w_key,
        grad_w_value,
        grad_w_out,
        grad_w_gate,
        grad_w_up,
        grad_w_down,
    )


def solution(mesh):
    placed = (
        P(("dp", "tensor"), None),
        P(),
        P(),
        P(None, "tensor"),
        P("tensor", None),
        P("tensor", None),
        P("tensor", None),
        P(None, "tensor", None),
        P(None, "tensor", None),
        P(None, "tensor", None),
        P("dp", None, None),
        P("dp", None, None),
        P(("dp", "tensor"), None),
    )
    return jax.shard_map(
        per_device,
        mesh=mesh,
        in_specs=placed,
        out_specs=(
            P(("dp", "tensor"), None),
            P("dp", None),
            P(),
            P(),
            P(None, "tensor"),
            P("tensor", None),
            P("tensor", None),
            P("tensor", None),
            P(None, "tensor", None),
            P(None, "tensor", None),
            P(None, "tensor", None),
        ),
        check_vma=False,
    )
```

profile of v0, /device:TPU:0, one launch (start us, length us, event | category | flops | bytes accessed | tf_op | source)
XLA Modules:
  0.0 3397.9 jit_solution(16931180885736290006)
XLA Ops:
  9.8 59.3 %all-gather.9.cloned.1.call-done = bf16[2048,1024]{1,0:T(8,128)(2,1)} async-done(((bf16[1024,1024]{1,0:T(8,128)(2,1)}), bf16[2048,1024]{1,0:T(8,128)(2,1)}) %all-gather.9.cloned.1.call-update) | async-done | bytes 4194320 | tf_op jit(solution)/shard_map/all_gather | solution.py:132
  109.0 92.2 %while.52 = (s32[]{:T(128)}, bf16[2,1024,4,2,64]{1,4,3,2,0:T(8,128)(2,1)S(1)}, f32[2,4,2,1024]{3,2,1,0:T(2,128)S(1)}, bf16[2,1024,4,64]{1,3,2,0:T(8,128)(2,1)}, ...) while((s32[]{:T(128)}, bf16[2,1024,4,2,64]{1,4,3,2,0:T(8,128)(2,1)S(1)}, ...), condition=%wide.region_4.5_spmd, body=%wide.region_1.4_spmd.sunk | while | flops 2249711616 | bytes 108267600 | solution.py:155
  109.3 15.8 fusion.206
  139.3 15.5 fusion.208
  155.2 15.8 fusion.206
  211.9 98.6 %reduce-scatter.8.cloned.1.call-done = f32[1024,1024]{1,0:T(8,128)} async-done(((f32[2048,1024]{1,0:T(8,128)}), f32[1024,1024]{1,0:T(8,128)}) %reduce-scatter.8.cloned.1.call-update) | async-done | bytes 4194320 | tf_op jit(solution)/shard_map/reduce_scatter | solution.py:158
  317.2 51.8 %all-gather.13.cloned.1.call-done = bf16[2048,1024]{1,0:T(8,128)(2,1)} async-done(((bf16[1024,1024]{1,0:T(8,128)(2,1)}), bf16[2048,1024]{1,0:T(8,128)(2,1)}) %all-gather.13.cloned.1.call-update) | async-done | bytes 4194320 | tf_op jit(solution)/shard_map/all_gather | solution.py:187
  368.9 58.8 %all-gather.11.cloned.1.call-done = bf16[2048,1024]{1,0:T(8,128)(2,1)} async-done(((bf16[1024,1024]{1,0:T(8,128)(2,1)}), bf16[2048,1024]{1,0:T(8,128)(2,1)}) %all-gather.11.cloned.1.call-update) | async-done | bytes 4194320 | tf_op jit(solution)/shard_map/all_gather | solution.py:161
  432.2 820.3 %while.54 = (s32[]{:T(128)}, f32[2048,1024]{1,0:T(8,128)}, bf16[4,8,256,1024]{3,2,1,0:T(8,128)(2,1)}, bf16[4,8,256,1024]{3,2,1,0:T(8,128)(2,1)}, bf16[4,8,256,10...) while((s32[]{:T(128)}, f32[2048,1024]{1,0:T(8,128)}, ...), condition=%wide.region_13.14_spmd, body=%wide.region_11.13_spmd.sunk | while | flops 21541720064 | bytes 387395840 | solution.py:228
  435.2 28.4 gather_fusion.2
  463.6 28.4 gather_fusion.1
  566.3 19.4 convolution_add_fusion.2
  585.8 51.6 %scatter_fusion.1 = f32[2048,1024]{1,0:T(8,128)} fusion(f32[2048,1024]{1,0:T(8,128)} %get-tuple-element.630, s32[5120]{0:T(1024)S(1)} %bitcast.412, f32[5120,1024]{1,0:T(8,128)} %bitcast.389), kind=kCustom, calls=%fused_computation.4.clone.1 | custom fusion | flops 5242880 | bytes 62935040 | tf_op jit(solution)/shard_map/while/body/eval_jaxpr/scatter-add | solution.py:224
  640.2 28.4 gather_fusion.2
  668.7 28.4 gather_fusion.1
  771.2 19.4 convolution_add_fusion.2
  790.7 51.6 %scatter_fusion.1 = f32[2048,1024]{1,0:T(8,128)} fusion(f32[2048,1024]{1,0:T(8,128)} %get-tuple-element.630, s32[5120]{0:T(1024)S(1)} %bitcast.412, f32[5120,1024]{1,0:T(8,128)} %bitcast.389), kind=kCustom, calls=%fused_computation.4.clone.1 | custom fusion | flops 5242880 | bytes 62935040 | tf_op jit(solution)/shard_map/while/body/eval_jaxpr/scatter-add | solution.py:224
  845.1 28.4 gather_fusion.2
  873.5 28.4 gather_fusion.1
  976.2 19.4 convolution_add_fusion.2
  995.6 51.6 %scatter_fusion.1 = f32[2048,1024]{1,0:T(8,128)} fusion(f32[2048,1024]{1,0:T(8,128)} %get-tuple-element.630, s32[5120]{0:T(1024)S(1)} %bitcast.412, f32[5120,1024]{1,0:T(8,128)} %bitcast.389), kind=kCustom, calls=%fused_computation.4.clone.1 | custom fusion | flops 5242880 | bytes 62935040 | tf_op jit(solution)/shard_map/while/body/eval_jaxpr/scatter-add | solution.py:224
  1050.1 28.4 gather_fusion.2
  1078.5 28.4 gather_fusion.1
  1181.0 19.4 convolution_add_fusion.2
  1200.5 51.6 %scatter_fusion.1 = f32[2048,1024]{1,0:T(8,128)} fusion(f32[2048,1024]{1,0:T(8,128)} %get-tuple-element.630, s32[5120]{0:T(1024)S(1)} %bitcast.412, f32[5120,1024]{1,0:T(8,128)} %bitcast.389), kind=kCustom, calls=%fused_computation.4.clone.1 | custom fusion | flops 5242880 | bytes 62935040 | tf_op jit(solution)/shard_map/while/body/eval_jaxpr/scatter-add | solution.py:224
  1258.6 54.4 %reduce-scatter.12.cloned.1.call-done = bf16[1024,1024]{1,0:T(8,128)(2,1)} async-done(((bf16[2048,1024]{1,0:T(8,128)(2,1)}), bf16[1024,1024]{1,0:T(8,128)(2,1)}) %reduce-scatter.12.cloned.1.call-update) | async-done | bytes 2097168 | tf_op jit(solution)/shard_map/reduce_scatter | solution.py:258
  1322.2 56.8 %all-gather.15.cloned.1.call-done = bf16[2048,1024]{1,0:T(8,128)(2,1)} async-done(((bf16[1024,1024]{1,0:T(8,128)(2,1)}), bf16[2048,1024]{1,0:T(8,128)(2,1)}) %all-gather.15.cloned.1.call-update) | async-done | bytes 4194320 | tf_op jit(solution)/shard_map/all_gather | solution.py:265
  1397.8 333.4 %while.55 = (s32[]{:T(128)}, f32[2,1024,4,2,64]{1,0,4,3,2:T(2,128)}, f32[2,1024,4,64]{1,0,3,2:T(2,128)}, bf16[2,1024,4,64]{1,3,2,0:T(8,128)(2,1)}, bf16[2,1024,4...) while((s32[]{:T(128)}, ...), condition=%wide.region_18.19_spmd, body=%wide.region_16.18_spmd.sunk | while | flops 5496365056 | bytes 282823840 | solution.py:273
  1398.3 17.6 fusion.239
  1415.9 15.8 fusion.243
  1431.6 24.7 fusion.240
  1456.4 28.1 fusion.241
  1509.0 18.8 dynamic_update_slice.50
  1527.8 36.6 %dynamic_update_slice.49 = f32[2,1024,4,2,64]{1,0,4,3,2:T(2,128)} dynamic-update-slice(f32[2,1024,4,2,64]{1,0,4,3,2:T(2,128)} %get-tuple-element.667, f32[1,1024,4,2,64]{1,0,4,3,2:T(1,128)S(1)} %copy.117, s32[]{:T(128)S(6)} %copy.157, s32[]{:T(128)} %constant.123.clone.1..sunk, s32[]{:T(128)} %constant.123.clone.1..sunk, s32[]{:T(128)} %constant.123.clone.1..sunk, s32[]{:T(128)} %constant.123.clone.1..sunk) | dynamic-update-slice | bytes 4194308 | tf_op jit(solution)/shard_map/while/body/jit(dynamic_update_index_in_dim)/dynamic_update_slice | solution.py:273
  1564.7 17.6 fusion.239
  1582.3 15.8 fusion.243
  1598.1 24.7 fusion.240
  1622.8 28.1 fusion.241
  1675.5 18.8 dynamic_update_slice.50
  1694.2 36.6 %dynamic_update_slice.49 = f32[2,1024,4,2,64]{1,0,4,3,2:T(2,128)} dynamic-update-slice(f32[2,1024,4,2,64]{1,0,4,3,2:T(2,128)} %get-tuple-element.667, f32[1,1024,4,2,64]{1,0,4,3,2:T(1,128)S(1)} %copy.117, s32[]{:T(128)S(6)} %copy.157, s32[]{:T(128)} %constant.123.clone.1..sunk, s32[]{:T(128)} %constant.123.clone.1..sunk, s32[]{:T(128)} %constant.123.clone.1..sunk, s32[]{:T(128)} %constant.123.clone.1..sunk) | dynamic-update-slice | bytes 4194308 | tf_op jit(solution)/shard_map/while/body/jit(dynamic_update_index_in_dim)/dynamic_update_slice | solution.py:273
  1769.2 432.4 %while.53 = (s32[]{:T(128)}, f32[2048,1024]{1,0:T(8,128)}, s32[4,8,640]{2,1,0:T(8,128)}, bf16[2048,1024]{1,0:T(8,128)(2,1)}, bf16[4,8,256,1024]{3,2,1,0:T(8,128)...) while((s32[]{:T(128)}, f32[2048,1024]{1,0:T(8,128)}, ...), condition=%wide.region_9.10_spmd, body=%wide.region_7.9_spmd.sunk | while | flops 8071449600 | bytes 149247088 | solution.py:178
  1771.7 28.4 gather_fusion
  1826.0 51.6 %scatter_fusion = f32[2048,1024]{1,0:T(8,128)} fusion(f32[2048,1024]{1,0:T(8,128)} %get-tuple-element.698, s32[5120]{0:T(1024)S(1)} %bitcast.413, f32[5120,1024]{1,0:T(8,128)} %bitcast.390), kind=kCustom, calls=%fused_computation.3.clone.1 | custom fusion | flops 5242880 | bytes 62935040 | tf_op jit(solution)/shard_map/while/body/eval_jaxpr/scatter-add | solution.py:175
  1879.8 28.4 gather_fusion
  1933.9 51.6 %scatter_fusion = f32[2048,1024]{1,0:T(8,128)} fusion(f32[2048,1024]{1,0:T(8,128)} %get-tuple-element.698, s32[5120]{0:T(1024)S(1)} %bitcast.413, f32[5120,1024]{1,0:T(8,128)} %bitcast.390), kind=kCustom, calls=%fused_computation.3.clone.1 | custom fusion | flops 5242880 | bytes 62935040 | tf_op jit(solution)/shard_map/while/body/eval_jaxpr/scatter-add | solution.py:175
  1987.8 28.4 gather_fusion
  2041.9 51.6 %scatter_fusion = f32[2048,1024]{1,0:T(8,128)} fusion(f32[2048,1024]{1,0:T(8,128)} %get-tuple-element.698, s32[5120]{0:T(1024)S(1)} %bitcast.413, f32[5120,1024]{1,0:T(8,128)} %bitcast.390), kind=kCustom, calls=%fused_computation.3.clone.1 | custom fusion | flops 5242880 | bytes 62935040 | tf_op jit(solution)/shard_map/while/body/eval_jaxpr/scatter-add | solution.py:175
  2095.8 28.4 gather_fusion
  2150.0 51.6 %scatter_fusion = f32[2048,1024]{1,0:T(8,128)} fusion(f32[2048,1024]{1,0:T(8,128)} %get-tuple-element.698, s32[5120]{0:T(1024)S(1)} %bitcast.413, f32[5120,1024]{1,0:T(8,128)} %bitcast.390), kind=kCustom, calls=%fused_computation.3.clone.1 | custom fusion | flops 5242880 | bytes 62935040 | tf_op jit(solution)/shard_map/while/body/eval_jaxpr/scatter-add | solution.py:175
  2207.7 24.1 copy.76
  2231.9 24.4 copy.74
  2256.3 24.5 copy.75
  2310.2 135.2 %reduce-scatter.20.cloned.1.call-done = bf16[32,256,64]{1,0,2:T(8,128)(2,1)} async-done(((bf16[32,256,1024]{1,0,2:T(8,128)(2,1)}), bf16[32,256,64]{1,0,2:T(8,128)(2,1)}) %reduce-scatter.20.cloned.1.call-update) | async-done | bytes 1048592 | tf_op jit(solution)/shard_map/reduce_scatter | solution.py:243
  2445.4 182.1 %reduce-scatter.16.cloned.1.call-done = bf16[32,256,64]{1,0,2:T(8,128)(2,1)} async-done(((bf16[32,256,1024]{1,0,2:T(8,128)(2,1)}), bf16[32,256,64]{1,0,2:T(8,128)(2,1)}) %reduce-scatter.16.cloned.1.call-update) | async-done | bytes 1048592 | tf_op jit(solution)/shard_map/reduce_scatter | solution.py:237
  2627.6 182.2 %reduce-scatter.18.cloned.1.call-done = bf16[32,256,64]{1,0,2:T(8,128)(2,1)} async-done(((bf16[32,256,1024]{1,0,2:T(8,128)(2,1)}), bf16[32,256,64]{1,0,2:T(8,128)(2,1)}) %reduce-scatter.18.cloned.1.call-update) | async-done | bytes 1048592 | tf_op jit(solution)/shard_map/reduce_scatter | solution.py:240
  2816.2 31.2 psum.35
  2848.0 69.6 %all-reduce.4.cloned.1.call-done = (bf16[1024,512]{1,0:T(8,128)(2,1)}, bf16[256,1024]{1,0:T(8,128)(2,1)}, bf16[256,1024]{1,0:T(8,128)(2,1)}, bf16[512,1024]{1,0:T(8,128)(2,1)}) async-done(((bf16[1024,512]{1,0:T(8,128)(2,1)}, bf16[256,1024]{1,0:T(8,128)(2,1)}, bf16[256,1024]{1,0:T(8,128)(2,1)}, bf16[512,1024]{1,0:T(8,128)(2,1)}), (bf16[1024,512]{1,0:T(8,128)(2,1)}, bf16[256,1024]{1,0:T(8,128)(2,1)}, ...) | async-done | bytes 3145744 | tf_op jit(solution)/shard_map/psum | solution.py:305
  2925.3 50.2 %all-gather.17.cloned.1.call-done = bf16[2048,1024]{1,0:T(8,128)(2,1)} async-done(((bf16[1024,1024]{1,0:T(8,128)(2,1)}), bf16[2048,1024]{1,0:T(8,128)(2,1)}) %all-gather.17.cloned.1.call-update) | async-done | bytes 4194320 | tf_op jit(solution)/shard_map/all_gather | solution.py:303
  2975.6 128.9 %all-gather.23.cloned.1.call-done = bf16[32,256,1024]{1,0,2:T(8,128)(2,1)} async-done(((bf16[32,256,64]{1,0,2:T(8,128)(2,1)}), bf16[32,256,1024]{1,0,2:T(8,128)(2,1)}) %all-gather.23.cloned.1.call-update) | async-done | bytes 16777232 | tf_op jit(solution)/shard_map/all_gather | solution.py:254
  3104.5 27.8 copy.79
  3132.3 99.4 %all-gather.19.cloned.1.call-done = bf16[32,256,1024]{1,0,2:T(8,128)(2,1)} async-done(((bf16[32,256,64]{1,0,2:T(8,128)(2,1)}), bf16[32,256,1024]{1,0,2:T(8,128)(2,1)}) %all-gather.19.cloned.1.call-update) | async-done | bytes 16777232 | tf_op jit(solution)/shard_map/all_gather | solution.py:248
  3231.6 27.8 copy.77
  3259.4 99.3 %all-gather.21.cloned.1.call-done = bf16[32,256,1024]{1,0,2:T(8,128)(2,1)} async-done(((bf16[32,256,64]{1,0,2:T(8,128)(2,1)}), bf16[32,256,1024]{1,0,2:T(8,128)(2,1)}) %all-gather.21.cloned.1.call-update) | async-done | bytes 16777232 | tf_op jit(solution)/shard_map/all_gather | solution.py:251
  3358.7 27.5 copy.78
  (367 shorter events, 705.1 us)
Async XLA Ops:
  7.2 198.1 %copy-start = (bf16[512,1024]{1,0:T(8,128)(2,1)S(1)}, bf16[512,1024]{1,0:T(8,128)(2,1)}, u32[]{:S(2)}) copy-start(bf16[512,1024]{1,0:T(8,128)(2,1)} %param.27) | copy-start | bytes 3145732
  7.2 65.1 %copy-start.51 = (f32[1024]{0:T(1024)S(1)}, f32[1024]{0:T(1024)}, u32[]{:S(2)}) copy-start(f32[1024]{0:T(1024)} %param.22) | copy-start | bytes 12292
  7.2 61.9 %all-gather.9.cloned.1.call-start = ((), (), s32[]{:S(2)}) async-start(), calls=%async_computation.7 | async-start | bytes 6291456 | tf_op jit(solution)/shard_map/all_gather | solution.py:132
  7.9 302.6 %reduce-scatter.8.cloned.1.call-start = ((), (), s32[]{:S(2)}) async-start(), calls=%async_computation.8 | async-start | bytes 12582912 | tf_op jit(solution)/shard_map/reduce_scatter | solution.py:158
  9.8 88.0 %copy-start.13 = (f32[2048,32]{0,1:T(8,128)}, f32[2048,32]{0,1:T(8,128)S(1)}, u32[]{:S(2)}) copy-start(f32[2048,32]{0,1:T(8,128)S(1)} %get-tuple-element.362) | copy-start | bytes 786436
  83.8 3.6 copy-start.15
  89.3 3.7 copy-start.56
  211.1 99.4 %copy-start.10 = (bf16[1024,1024]{1,0:T(8,128)(2,1)S(1)}, bf16[1024,1024]{1,0:T(8,128)(2,1)}, u32[]{:S(2)}) copy-start(bf16[1024,1024]{1,0:T(8,128)(2,1)} %param.21) | copy-start | bytes 6291460
  211.1 157.8 %all-gather.13.cloned.1.call-start = ((), (), s32[]{:S(2)}) async-start(), calls=%async_computation.11 | async-start | bytes 6291456 | tf_op jit(solution)/shard_map/all_gather | solution.py:187
  211.9 103.5 %copy-start.44 = (f32[1024]{0:T(1024)S(1)}, f32[1024]{0:T(1024)}, u32[]{:S(2)}) copy-start(f32[1024]{0:T(1024)} %param.23) | copy-start | bytes 12292
  211.9 215.9 %all-gather.11.cloned.1.call-start = ((), (), s32[]{:S(2)}) async-start(), calls=%async_computation.9 | async-start | bytes 6291456 | tf_op jit(solution)/shard_map/all_gather | solution.py:161
  317.1 995.9 %reduce-scatter.12.cloned.1.call-start = ((), (), s32[]{:S(2)}) async-start(), calls=%async_computation.12 | async-start | bytes 6291456 | tf_op jit(solution)/shard_map/reduce_scatter | solution.py:258
  492.0 10.5 copy-start.2
  535.3 10.4 copy-start.4
  545.7 9.4 copy-start.3
  566.3 19.4 copy-start.30
  697.1 10.5 copy-start.2
  740.2 10.4 copy-start.4
  750.6 9.3 copy-start.3
  771.2 19.4 copy-start.30
  902.0 10.5 copy-start.2
  945.2 10.4 copy-start.4
  955.6 9.4 copy-start.3
  976.2 19.4 copy-start.30
  1107.0 10.5 copy-start.2
  1150.1 10.4 copy-start.4
  1160.4 9.3 copy-start.3
  1181.0 19.4 copy-start.30
  1258.5 54.5 %copy-start.39 = (f32[1024]{0:T(1024)S(1)}, f32[1024]{0:T(1024)}, u32[]{:S(2)}) copy-start(f32[1024]{0:T(1024)} %copy-done.38) | copy-start | bytes 12292
  1258.5 54.5 %copy-start.45 = (f32[1024]{0:T(1024)S(1)}, f32[1024]{0:T(1024)}, u32[]{:S(2)}) copy-start(f32[1024]{0:T(1024)} %param.23) | copy-start | bytes 12292
  1258.5 59.9 %copy-start.12 = (bf16[1024,1024]{1,0:T(8,128)(2,1)S(1)}, bf16[1024,1024]{1,0:T(8,128)(2,1)}, u32[]{:S(2)}) copy-start(bf16[1024,1024]{1,0:T(8,128)(2,1)} %param.33) | copy-start | bytes 6291460
  1258.6 59.9 %copy-start.47 = (f32[1024]{0:T(1024)S(1)}, f32[1024]{0:T(1024)}, u32[]{:S(2)}) copy-start(f32[1024]{0:T(1024)} %get-tuple-element.366) | copy-start | bytes 12292
  1258.6 120.4 %all-gather.15.cloned.1.call-start = ((), (), s32[]{:S(2)}) async-start(), calls=%async_computation.13 | async-start | bytes 6291456 | tf_op jit(solution)/shard_map/all_gather | solution.py:265
  1313.0 5.5 copy-start.6
  1322.1 976.1 %reduce-scatter.14.cloned.1.call-start = ((), (), s32[]{:S(2)}) async-start(), calls=%async_computation.14 | async-start | bytes 6291456 | tf_op jit(solution)/shard_map/reduce_scatter | solution.py:292
  1387.1 10.6 copy-start.37
  1731.2 6.7 copy-start.14
  1731.2 6.7 copy-start.16
  1749.0 5.9 copy-start.25
  1749.0 5.8 copy-start.28
  1749.0 5.8 copy-start.29
  1749.0 5.9 copy-start.32
  1764.8 537.2 %reduce-scatter.10.cloned.1.call-start = ((), (), s32[]{:S(2)}) async-start(), calls=%async_computation.10 | async-start | bytes 6291456 | tf_op jit(solution)/shard_map/reduce_scatter | solution.py:183
  2207.7 237.7 %reduce-scatter.20.cloned.1.call-start = ((), (), s32[]{:S(2)}) async-start(), calls=%async_computation.20 | async-start | bytes 17825792 | tf_op jit(solution)/shard_map/reduce_scatter | solution.py:243
  2231.8 395.7 %reduce-scatter.16.cloned.1.call-start = ((), (), s32[]{:S(2)}) async-start(), calls=%async_computation.16 | async-start | bytes 17825792 | tf_op jit(solution)/shard_map/reduce_scatter | solution.py:237
  2256.3 553.5 %reduce-scatter.18.cloned.1.call-start = ((), (), s32[]{:S(2)}) async-start(), calls=%async_computation.18 | async-start | bytes 17825792 | tf_op jit(solution)/shard_map/reduce_scatter | solution.py:240
  2280.9 7.7 copy-start.18
  2280.9 636.7 %all-reduce.4.cloned.1.call-start = ((), (), s32[]{:S(2)}) async-start(), calls=%async_computation.22 | async-start | bytes 6291456 | tf_op jit(solution)/shard_map/psum | solution.py:305
  2281.6 7.0 copy-start.22
  2290.7 4.0 copy-start.55
  2298.1 4.0 copy-start.40
  2298.1 4.0 copy-start.46
  2298.1 4.0 copy-start.48
  2298.1 4.0 copy-start.50
  2298.1 677.4 %all-gather.17.cloned.1.call-start = ((), (), s32[]{:S(2)}) async-start(), calls=%async_computation.15 | async-start | bytes 6291456 | tf_op jit(solution)/shard_map/all_gather | solution.py:303
  2310.1 499.8 %copy-start.58 = (u32[32]{0:T(128)S(1)}, u32[32]{0:T(128)}, u32[]{:S(2)}) copy-start(u32[32]{0:T(128)} %constant.138) | copy-start | bytes 388
  2310.1 500.4 %copy-start.53 = (bf16[1024]{0:T(1024)(128)(2,1)S(1)}, bf16[1024]{0:T(1024)(128)(2,1)}, u32[]{:S(2)}) copy-start(bf16[1024]{0:T(1024)(128)(2,1)} %get-tuple-element.266) | copy-start | bytes 6148
  2310.1 500.4 %copy-start.54 = (bf16[1024]{0:T(1024)(128)(2,1)S(1)}, bf16[1024]{0:T(1024)(128)(2,1)}, u32[]{:S(2)}) copy-start(bf16[1024]{0:T(1024)(128)(2,1)} %get-tuple-element.350) | copy-start | bytes 6148
  2310.1 794.4 %all-gather.23.cloned.1.call-start = ((), (), s32[]{:S(2)}) async-start(), calls=%async_computation.21 | async-start | bytes 17825792 | tf_op jit(solution)/shard_map/all_gather | solution.py:254
  2445.4 786.2 %all-gather.19.cloned.1.call-start = ((), (), s32[]{:S(2)}) async-start(), calls=%async_computation.17 | async-start | bytes 17825792 | tf_op jit(solution)/shard_map/all_gather | solution.py:248
  2627.6 731.2 %all-gather.21.cloned.1.call-start = ((), (), s32[]{:S(2)}) async-start(), calls=%async_computation.19 | async-start | bytes 17825792 | tf_op jit(solution)/shard_map/all_gather | solution.py:251
  2917.6 5.1 copy-start.35
  2917.6 6.2 copy-start.31
  3386.2 4.7 copy-start.1
  (24 other events, 52.8 us)
Sparse Core Ops, SparseCore 0:
  9.6 59.4 all-gather.8
  211.3 99.2 reduce-scatter.7
  312.2 56.7 all-gather.12
  371.0 56.7 all-gather.10
  1258.7 54.3 reduce-scatter.11
  1322.2 56.7 all-gather.14
  1764.9 54.2 reduce-scatter.13
  2207.8 54.7 reduce-scatter.9
  2266.7 178.6 reduce-scatter.19
  2449.9 177.5 reduce-scatter.15
  2632.2 177.5 reduce-scatter.17
  2814.7 102.8 all-reduce.3
  2919.7 55.7 all-gather.16
  2977.6 126.8 all-gather.22
  3106.5 125.0 all-gather.18
  3233.6 125.0 all-gather.20
where the time goes:
time: 3420 us; the launch traced here: 3400 us
  waiting for transfers between devices  1330 us (39%)
  matrix products  749 us (22%)
  local copies, waits for them, and re-layouts  697 us (20%)
  other arithmetic  570 us (17%)
  blocking collectives  36.2 us (1%)
    scatter-add x4, other arithmetic, expert_backward(): running.at[slot_part.reshape(-1)].add(grad_gathered.reshape(-1, width))  206 us
    scatter-add x4, other arithmetic, expert_forward(): running.at[slot_part.reshape(-1)].add(expert_out.reshape(-1, width))  206 us
    reduce_scatter x1, waiting for transfers between devices, per_device(): lax.psum_scatter(grad_w_up.astype(jnp.bfloat16), 'dp', scatter_dimension=...  182 us
    reduce_scatter x1, waiting for transfers between devices, per_device(): lax.psum_scatter(grad_w_gate.astype(jnp.bfloat16), 'dp', scatter_dimensio...  182 us
    reduce_scatter x1, waiting for transfers between devices, per_device(): lax.psum_scatter(grad_w_down.astype(jnp.bfloat16), 'dp', scatter_dimensio...  135 us
    all_gather x1, waiting for transfers between devices, per_device(): lax.all_gather(shared[2].astype(jnp.bfloat16), 'dp', axis=2, tiled=True)  129 us
    dynamic_update_slice x8, local copies, waits for them, and re-layouts, per_device(): lax.map(attend_backward, (seq_queries, seq_keys, seq_values, grad_mixed,...  117 us
    gather x4, local copies, waits for them, and re-layouts, expert_backward(): grad_full[slot_part].astype(jnp.float32) * weight_part[..., None]  114 us
  transfers between devices with their start and end apart: 16, of which 14 were waited for; matrix products, arithmetic and copies ran while one was open for 18% of the time, Pallas kernels for 0%

commit v1 on v0

--- a/solution.py
+++ b/solution.py
@@ -302,7 +302,9 @@
     )
     grad_tokens = lax.all_gather(grad_input.astype(jnp.bfloat16), "tensor", axis=0, tiled=True)
     grad_w_query, grad_w_key, grad_w_value, grad_w_out, gains_total = (
-        lax.psum(grad_w_query.astype(jnp.bfloat16), "dp").astype(jnp.float32),
+        jnp.sum(lax.all_gather(grad_w_query.astype(jnp.bfloat16), axis_name="dp"), 0).astype(
+            jnp.float32
+        ),
         lax.psum(grad_w_key.astype(jnp.bfloat16), "dp").astype(jnp.float32),
         lax.psum(grad_w_value.astype(jnp.bfloat16), "dp").astype(jnp.float32),
         lax.psum(grad_w_out.astype(jnp.bfloat16), "dp").astype(jnp.float32),

time: 3420 us -> 3540 us (1.035)
  waiting for transfers between devices: 1330 us -> 1440 us
    all_gather x0 -> x1, waiting for transfers between devices: none -> 130 us  [per_device(): lax.all_gather(grad_w_query.astype(jnp.bfloat16), axis_name='dp')]
    unnamed x116 -> x110, local copies, waits for them, and re-layouts: 102 us -> 102 us
  transfers between devices with their start and end apart: 16 -> 17, of which waited for: 14 -> 15; matrix products, arithmetic and copies ran while one was open for 18% -> 18% of each run, Pallas kernels for 0% -> 0%
where the time goes in v1:
time: 3540 us; the launch traced here: 3520 us
  waiting for transfers between devices  1440 us (41%)
  matrix products  751 us (21%)
  local copies, waits for them, and re-layouts  697 us (20%)
  other arithmetic  580 us (16%)
  blocking collectives  36 us (1%)
    scatter-add x4, other arithmetic, expert_backward(): running.at[slot_part.reshape(-1)].add(grad_gathered.reshape(-1, width))  206 us
    scatter-add x4, other arithmetic, expert_forward(): running.at[slot_part.reshape(-1)].add(expert_out.reshape(-1, width))  206 us
    reduce_scatter x1, waiting for transfers between devices, per_device(): lax.psum_scatter(grad_w_up.astype(jnp.bfloat16), 'dp', scatter_dimension=...  182 us
    reduce_scatter x1, waiting for transfers between devices, per_device(): lax.psum_scatter(grad_w_gate.astype(jnp.bfloat16), 'dp', scatter_dimensio...  182 us
    reduce_scatter x1, waiting for transfers between devices, per_device(): lax.psum_scatter(grad_w_down.astype(jnp.bfloat16), 'dp', scatter_dimensio...  133 us
    all_gather x1, waiting for transfers between devices, per_device(): lax.all_gather(grad_w_query.astype(jnp.bfloat16), axis_name='dp')  130 us
    dynamic_update_slice x8, local copies, waits for them, and re-layouts, per_device(): lax.map(attend_backward, (seq_queries, seq_keys, seq_values, grad_mixed,...  117 us
    all_gather x1, waiting for transfers between devices, per_device(): lax.all_gather(shared[2].astype(jnp.bfloat16), 'dp', axis=2, tiled=True)  116 us
  transfers between devices with their start and end apart: 17, of which 15 were waited for; matrix products, arithmetic and copies ran while one was open for 18% of the time, Pallas kernels for 0%

profile of v1, /device:TPU:0, one launch (start us, length us, event | category | flops | bytes accessed | tf_op | source)
XLA Modules:
  0.0 3520.8 jit_solution(3230595662735450194)
XLA Ops:
  9.8 59.3 %all-gather.11.cloned.1.call-done = bf16[2048,1024]{1,0:T(8,128)(2,1)} async-done(((bf16[1024,1024]{1,0:T(8,128)(2,1)}), bf16[2048,1024]{1,0:T(8,128)(2,1)}) %all-gather.11.cloned.1.call-update) | async-done | bytes 4194320 | tf_op jit(solution)/shard_map/all_gather | solution.py:132
  108.9 92.2 %while.52 = (s32[]{:T(128)}, bf16[2,1024,4,2,64]{1,4,3,2,0:T(8,128)(2,1)S(1)}, f32[2,4,2,1024]{3,2,1,0:T(2,128)S(1)}, bf16[2,1024,4,64]{1,3,2,0:T(8,128)(2,1)}, ...) while((s32[]{:T(128)}, bf16[2,1024,4,2,64]{1,4,3,2,0:T(8,128)(2,1)S(1)}, ...), condition=%wide.region_4.5_spmd, body=%wide.region_1.4_spmd.sunk | while | flops 2249711616 | bytes 108267600 | solution.py:155
  109.2 15.8 fusion.206
  155.1 15.8 fusion.206
  211.8 98.6 %reduce-scatter.8.cloned.1.call-done = f32[1024,1024]{1,0:T(8,128)} async-done(((f32[2048,1024]{1,0:T(8,128)}), f32[1024,1024]{1,0:T(8,128)}) %reduce-scatter.8.cloned.1.call-update) | async-done | bytes 4194320 | tf_op jit(solution)/shard_map/reduce_scatter | solution.py:158
  317.2 51.7 %all-gather.15.cloned.1.call-done = bf16[2048,1024]{1,0:T(8,128)(2,1)} async-done(((bf16[1024,1024]{1,0:T(8,128)(2,1)}), bf16[2048,1024]{1,0:T(8,128)(2,1)}) %all-gather.15.cloned.1.call-update) | async-done | bytes 4194320 | tf_op jit(solution)/shard_map/all_gather | solution.py:187
  368.9 58.8 %all-gather.13.cloned.1.call-done = bf16[2048,1024]{1,0:T(8,128)(2,1)} async-done(((bf16[1024,1024]{1,0:T(8,128)(2,1)}), bf16[2048,1024]{1,0:T(8,128)(2,1)}) %all-gather.13.cloned.1.call-update) | async-done | bytes 4194320 | tf_op jit(solution)/shard_map/all_gather | solution.py:161
  432.1 819.8 %while.54 = (s32[]{:T(128)}, f32[2048,1024]{1,0:T(8,128)}, bf16[4,8,256,1024]{3,2,1,0:T(8,128)(2,1)}, bf16[4,8,256,1024]{3,2,1,0:T(8,128)(2,1)}, bf16[4,8,256,10...) while((s32[]{:T(128)}, f32[2048,1024]{1,0:T(8,128)}, ...), condition=%wide.region_13.14_spmd, body=%wide.region_11.13_spmd.sunk | while | flops 21541720064 | bytes 387395840 | solution.py:228
  435.1 28.4 gather_fusion.2
  463.5 28.4 gather_fusion.1
  566.1 19.4 convolution_add_fusion.2
  585.6 51.6 %scatter_fusion.1 = f32[2048,1024]{1,0:T(8,128)} fusion(f32[2048,1024]{1,0:T(8,128)} %get-tuple-element.629, s32[5120]{0:T(1024)S(1)} %bitcast.414, f32[5120,1024]{1,0:T(8,128)} %bitcast.390), kind=kCustom, calls=%fused_computation.4.clone.1 | custom fusion | flops 5242880 | bytes 62935040 | tf_op jit(solution)/shard_map/while/body/eval_jaxpr/scatter-add | solution.py:224
  640.0 28.4 gather_fusion.2
  668.4 28.4 gather_fusion.1
  770.9 19.4 convolution_add_fusion.2
  790.3 51.6 %scatter_fusion.1 = f32[2048,1024]{1,0:T(8,128)} fusion(f32[2048,1024]{1,0:T(8,128)} %get-tuple-element.629, s32[5120]{0:T(1024)S(1)} %bitcast.414, f32[5120,1024]{1,0:T(8,128)} %bitcast.390), kind=kCustom, calls=%fused_computation.4.clone.1 | custom fusion | flops 5242880 | bytes 62935040 | tf_op jit(solution)/shard_map/while/body/eval_jaxpr/scatter-add | solution.py:224
  844.8 28.4 gather_fusion.2
  873.2 28.4 gather_fusion.1
  975.7 19.4 convolution_add_fusion.2
  995.2 51.6 %scatter_fusion.1 = f32[2048,1024]{1,0:T(8,128)} fusion(f32[2048,1024]{1,0:T(8,128)} %get-tuple-element.629, s32[5120]{0:T(1024)S(1)} %bitcast.414, f32[5120,1024]{1,0:T(8,128)} %bitcast.390), kind=kCustom, calls=%fused_computation.4.clone.1 | custom fusion | flops 5242880 | bytes 62935040 | tf_op jit(solution)/shard_map/while/body/eval_jaxpr/scatter-add | solution.py:224
  1049.6 28.4 gather_fusion.2
  1078.1 28.4 gather_fusion.1
  1180.5 19.4 convolution_add_fusion.2
  1199.9 51.6 %scatter_fusion.1 = f32[2048,1024]{1,0:T(8,128)} fusion(f32[2048,1024]{1,0:T(8,128)} %get-tuple-element.629, s32[5120]{0:T(1024)S(1)} %bitcast.414, f32[5120,1024]{1,0:T(8,128)} %bitcast.390), kind=kCustom, calls=%fused_computation.4.clone.1 | custom fusion | flops 5242880 | bytes 62935040 | tf_op jit(solution)/shard_map/while/body/eval_jaxpr/scatter-add | solution.py:224
  1258.1 54.4 %reduce-scatter.12.cloned.1.call-done = bf16[1024,1024]{1,0:T(8,128)(2,1)} async-done(((bf16[2048,1024]{1,0:T(8,128)(2,1)}), bf16[1024,1024]{1,0:T(8,128)(2,1)}) %reduce-scatter.12.cloned.1.call-update) | async-done | bytes 2097168 | tf_op jit(solution)/shard_map/reduce_scatter | solution.py:258
  1321.6 56.8 %all-gather.17.cloned.1.call-done = bf16[2048,1024]{1,0:T(8,128)(2,1)} async-done(((bf16[1024,1024]{1,0:T(8,128)(2,1)}), bf16[2048,1024]{1,0:T(8,128)(2,1)}) %all-gather.17.cloned.1.call-update) | async-done | bytes 4194320 | tf_op jit(solution)/shard_map/all_gather | solution.py:265
  1397.2 333.4 %while.55 = (s32[]{:T(128)}, f32[2,1024,4,2,64]{1,0,4,3,2:T(2,128)}, f32[2,1024,4,64]{1,0,3,2:T(2,128)}, bf16[2,1024,4,64]{1,3,2,0:T(8,128)(2,1)}, bf16[2,1024,4...) while((s32[]{:T(128)}, ...), condition=%wide.region_18.19_spmd, body=%wide.region_16.18_spmd.sunk | while | flops 5496365056 | bytes 282823840 | solution.py:273
  1397.7 17.6 fusion.239
  1415.3 15.8 fusion.243
  1431.1 24.7 fusion.240
  1455.8 28.1 fusion.241
  1508.5 18.8 dynamic_update_slice.50
  1527.3 36.6 %dynamic_update_slice.49 = f32[2,1024,4,2,64]{1,0,4,3,2:T(2,128)} dynamic-update-slice(f32[2,1024,4,2,64]{1,0,4,3,2:T(2,128)} %get-tuple-element.666, f32[1,1024,4,2,64]{1,0,4,3,2:T(1,128)S(1)} %copy.117, s32[]{:T(128)S(6)} %copy.157, s32[]{:T(128)} %constant.124.clone.1..sunk, s32[]{:T(128)} %constant.124.clone.1..sunk, s32[]{:T(128)} %constant.124.clone.1..sunk, s32[]{:T(128)} %constant.124.clone.1..sunk) | dynamic-update-slice | bytes 4194308 | tf_op jit(solution)/shard_map/while/body/jit(dynamic_update_index_in_dim)/dynamic_update_slice | solution.py:273
  1564.2 17.6 fusion.239
  1581.8 15.8 fusion.243
  1597.5 24.7 fusion.240
  1622.3 28.1 fusion.241
  1674.9 18.8 dynamic_update_slice.50
  1693.7 36.6 %dynamic_update_slice.49 = f32[2,1024,4,2,64]{1,0,4,3,2:T(2,128)} dynamic-update-slice(f32[2,1024,4,2,64]{1,0,4,3,2:T(2,128)} %get-tuple-element.666, f32[1,1024,4,2,64]{1,0,4,3,2:T(1,128)S(1)} %copy.117, s32[]{:T(128)S(6)} %copy.157, s32[]{:T(128)} %constant.124.clone.1..sunk, s32[]{:T(128)} %constant.124.clone.1..sunk, s32[]{:T(128)} %constant.124.clone.1..sunk, s32[]{:T(128)} %constant.124.clone.1..sunk) | dynamic-update-slice | bytes 4194308 | tf_op jit(solution)/shard_map/while/body/jit(dynamic_update_index_in_dim)/dynamic_update_slice | solution.py:273
  1768.7 432.4 %while.53 = (s32[]{:T(128)}, f32[2048,1024]{1,0:T(8,128)}, s32[4,8,640]{2,1,0:T(8,128)}, bf16[2048,1024]{1,0:T(8,128)(2,1)}, bf16[4,8,256,1024]{3,2,1,0:T(8,128)...) while((s32[]{:T(128)}, f32[2048,1024]{1,0:T(8,128)}, ...), condition=%wide.region_9.10_spmd, body=%wide.region_7.9_spmd.sunk | while | flops 8071449600 | bytes 149247088 | solution.py:178
  1771.1 28.4 gather_fusion
  1825.4 51.6 %scatter_fusion = f32[2048,1024]{1,0:T(8,128)} fusion(f32[2048,1024]{1,0:T(8,128)} %get-tuple-element.697, s32[5120]{0:T(1024)S(1)} %bitcast.415, f32[5120,1024]{1,0:T(8,128)} %bitcast.391), kind=kCustom, calls=%fused_computation.3.clone.1 | custom fusion | flops 5242880 | bytes 62935040 | tf_op jit(solution)/shard_map/while/body/eval_jaxpr/scatter-add | solution.py:175
  1879.3 28.4 gather_fusion
  1933.4 51.6 %scatter_fusion = f32[2048,1024]{1,0:T(8,128)} fusion(f32[2048,1024]{1,0:T(8,128)} %get-tuple-element.697, s32[5120]{0:T(1024)S(1)} %bitcast.415, f32[5120,1024]{1,0:T(8,128)} %bitcast.391), kind=kCustom, calls=%fused_computation.3.clone.1 | custom fusion | flops 5242880 | bytes 62935040 | tf_op jit(solution)/shard_map/while/body/eval_jaxpr/scatter-add | solution.py:175
  1987.3 28.4 gather_fusion
  2041.4 51.6 %scatter_fusion = f32[2048,1024]{1,0:T(8,128)} fusion(f32[2048,1024]{1,0:T(8,128)} %get-tuple-element.697, s32[5120]{0:T(1024)S(1)} %bitcast.415, f32[5120,1024]{1,0:T(8,128)} %bitcast.391), kind=kCustom, calls=%fused_computation.3.clone.1 | custom fusion | flops 5242880 | bytes 62935040 | tf_op jit(solution)/shard_map/while/body/eval_jaxpr/scatter-add | solution.py:175
  2095.2 28.4 gather_fusion
  2149.5 51.6 %scatter_fusion = f32[2048,1024]{1,0:T(8,128)} fusion(f32[2048,1024]{1,0:T(8,128)} %get-tuple-element.697, s32[5120]{0:T(1024)S(1)} %bitcast.415, f32[5120,1024]{1,0:T(8,128)} %bitcast.391), kind=kCustom, calls=%fused_computation.3.clone.1 | custom fusion | flops 5242880 | bytes 62935040 | tf_op jit(solution)/shard_map/while/body/eval_jaxpr/scatter-add | solution.py:175
  2207.2 24.1 copy.76
  2231.3 24.4 copy.74
  2255.8 24.5 copy.75
  2311.8 132.9 %reduce-scatter.20.cloned.1.call-done = bf16[32,256,64]{1,0,2:T(8,128)(2,1)} async-done(((bf16[32,256,1024]{1,0,2:T(8,128)(2,1)}), bf16[32,256,64]{1,0,2:T(8,128)(2,1)}) %reduce-scatter.20.cloned.1.call-update) | async-done | bytes 1048592 | tf_op jit(solution)/shard_map/reduce_scatter | solution.py:243
  2444.8 182.0 %reduce-scatter.16.cloned.1.call-done = bf16[32,256,64]{1,0,2:T(8,128)(2,1)} async-done(((bf16[32,256,1024]{1,0,2:T(8,128)(2,1)}), bf16[32,256,64]{1,0,2:T(8,128)(2,1)}) %reduce-scatter.16.cloned.1.call-update) | async-done | bytes 1048592 | tf_op jit(solution)/shard_map/reduce_scatter | solution.py:237
  2626.8 182.2 %reduce-scatter.18.cloned.1.call-done = bf16[32,256,64]{1,0,2:T(8,128)(2,1)} async-done(((bf16[32,256,1024]{1,0,2:T(8,128)(2,1)}), bf16[32,256,64]{1,0,2:T(8,128)(2,1)}) %reduce-scatter.18.cloned.1.call-update) | async-done | bytes 1048592 | tf_op jit(solution)/shard_map/reduce_scatter | solution.py:240
  2815.4 31.0 psum.28
  2847.0 64.4 %all-reduce.4.cloned.1.call-done = (bf16[256,1024]{1,0:T(8,128)(2,1)}, bf16[256,1024]{1,0:T(8,128)(2,1)}, bf16[512,1024]{1,0:T(8,128)(2,1)}) async-done(((bf16[256,1024]{1,0:T(8,128)(2,1)}, bf16[256,1024]{1,0:T(8,128)(2,1)}, bf16[512,1024]{1,0:T(8,128)(2,1)}), (bf16[256,1024]{1,0:T(8,128)(2,1)}, bf16[256,1024]{1,0:T(8,128)(2,1)}, bf16[512,1024]{1,0:T(8,128)(2,1)})) %all-reduce.4.cloned.1.call-update) | async-done | bytes 2097168 | tf_op jit(solution)/shard_map/psum | solution.py:308
  2918.4 51.5 %all-gather.19.cloned.1.call-done = bf16[2048,1024]{1,0:T(8,128)(2,1)} async-done(((bf16[1024,1024]{1,0:T(8,128)(2,1)}), bf16[2048,1024]{1,0:T(8,128)(2,1)}) %all-gather.19.cloned.1.call-update) | async-done | bytes 4194320 | tf_op jit(solution)/shard_map/all_gather | solution.py:303
  2969.9 129.7 %all-gather.27.cloned.1.call-done = bf16[16384,512]{1,0:T(8,128)(2,1)} async-done(((bf16[1024,512]{1,0:T(8,128)(2,1)}), bf16[16384,512]{1,0:T(8,128)(2,1)}) %all-gather.27.cloned.1.call-update) | async-done | bytes 16777232 | tf_op jit(solution)/shard_map/all_gather | solution.py:305
  3110.7 116.3 %all-gather.25.cloned.1.call-done = bf16[32,256,1024]{1,0,2:T(8,128)(2,1)} async-done(((bf16[32,256,64]{1,0,2:T(8,128)(2,1)}), bf16[32,256,1024]{1,0,2:T(8,128)(2,1)}) %all-gather.25.cloned.1.call-update) | async-done | bytes 16777232 | tf_op jit(solution)/shard_map/all_gather | solution.py:254
  3227.0 27.7 copy.79
  3254.7 99.5 %all-gather.21.cloned.1.call-done = bf16[32,256,1024]{1,0,2:T(8,128)(2,1)} async-done(((bf16[32,256,64]{1,0,2:T(8,128)(2,1)}), bf16[32,256,1024]{1,0,2:T(8,128)(2,1)}) %all-gather.21.cloned.1.call-update) | async-done | bytes 16777232 | tf_op jit(solution)/shard_map/all_gather | solution.py:248
  3354.2 27.7 copy.77
  3382.0 99.6 %all-gather.23.cloned.1.call-done = bf16[32,256,1024]{1,0,2:T(8,128)(2,1)} async-done(((bf16[32,256,64]{1,0,2:T(8,128)(2,1)}), bf16[32,256,1024]{1,0,2:T(8,128)(2,1)}) %all-gather.23.cloned.1.call-update) | async-done | bytes 16777232 | tf_op jit(solution)/shard_map/all_gather | solution.py:251
  3481.6 27.5 copy.78
  (365 shorter events, 732.6 us)
Async XLA Ops:
  7.2 198.0 %copy-start = (bf16[512,1024]{1,0:T(8,128)(2,1)S(1)}, bf16[512,1024]{1,0:T(8,128)(2,1)}, u32[]{:S(2)}) copy-start(bf16[512,1024]{1,0:T(8,128)(2,1)} %param.27) | copy-start | bytes 3145732
  7.2 65.1 %copy-start.48 = (f32[1024]{0:T(1024)S(1)}, f32[1024]{0:T(1024)}, u32[]{:S(2)}) copy-start(f32[1024]{0:T(1024)} %param.22) | copy-start | bytes 12292
  7.2 61.9 %all-gather.11.cloned.1.call-start = ((), (), s32[]{:S(2)}) async-start(), calls=%async_computation.7 | async-start | bytes 6291456 | tf_op jit(solution)/shard_map/all_gather | solution.py:132
  7.9 302.5 %reduce-scatter.8.cloned.1.call-start = ((), (), s32[]{:S(2)}) async-start(), calls=%async_computation.8 | async-start | bytes 12582912 | tf_op jit(solution)/shard_map/reduce_scatter | solution.py:158
  9.8 87.9 %copy-start.13 = (f32[2048,32]{0,1:T(8,128)}, f32[2048,32]{0,1:T(8,128)S(1)}, u32[]{:S(2)}) copy-start(f32[2048,32]{0,1:T(8,128)S(1)} %get-tuple-element.361) | copy-start | bytes 786436
  69.1 3.4 copy-start.8
  72.5 3.1 copy-start.31
  83.7 3.6 copy-start.15
  89.2 3.7 copy-start.53
  211.0 99.4 %copy-start.10 = (bf16[1024,1024]{1,0:T(8,128)(2,1)S(1)}, bf16[1024,1024]{1,0:T(8,128)(2,1)}, u32[]{:S(2)}) copy-start(bf16[1024,1024]{1,0:T(8,128)(2,1)} %param.21) | copy-start | bytes 6291460
  211.0 157.8 %all-gather.15.cloned.1.call-start = ((), (), s32[]{:S(2)}) async-start(), calls=%async_computation.11 | async-start | bytes 6291456 | tf_op jit(solution)/shard_map/all_gather | solution.py:187
  211.8 103.6 %copy-start.41 = (f32[1024]{0:T(1024)S(1)}, f32[1024]{0:T(1024)}, u32[]{:S(2)}) copy-start(f32[1024]{0:T(1024)} %param.23) | copy-start | bytes 12292
  211.8 215.9 %all-gather.13.cloned.1.call-start = ((), (), s32[]{:S(2)}) async-start(), calls=%async_computation.9 | async-start | bytes 6291456 | tf_op jit(solution)/shard_map/all_gather | solution.py:161
  317.1 995.4 %reduce-scatter.12.cloned.1.call-start = ((), (), s32[]{:S(2)}) async-start(), calls=%async_computation.12 | async-start | bytes 6291456 | tf_op jit(solution)/shard_map/reduce_scatter | solution.py:258
  492.0 10.5 copy-start.2
  535.1 10.4 copy-start.4
  545.5 9.3 copy-start.3
  566.1 19.4 copy-start.29
  696.9 10.5 copy-start.2
  739.9 10.4 copy-start.4
  750.3 9.3 copy-start.3
  770.9 19.4 copy-start.29
  901.6 10.5 copy-start.2
  944.8 10.4 copy-start.4
  955.2 9.3 copy-start.3
  975.7 19.4 copy-start.29
  1106.5 10.5 copy-start.2
  1149.5 10.4 copy-start.4
  1159.9 9.3 copy-start.3
  1180.5 19.4 copy-start.29
  1258.0 54.5 %copy-start.36 = (f32[1024]{0:T(1024)S(1)}, f32[1024]{0:T(1024)}, u32[]{:S(2)}) copy-start(f32[1024]{0:T(1024)} %copy-done.35) | copy-start | bytes 12292
  1258.0 54.5 %copy-start.42 = (f32[1024]{0:T(1024)S(1)}, f32[1024]{0:T(1024)}, u32[]{:S(2)}) copy-start(f32[1024]{0:T(1024)} %param.23) | copy-start | bytes 12292
  1258.0 59.9 %copy-start.12 = (bf16[1024,1024]{1,0:T(8,128)(2,1)S(1)}, bf16[1024,1024]{1,0:T(8,128)(2,1)}, u32[]{:S(2)}) copy-start(bf16[1024,1024]{1,0:T(8,128)(2,1)} %param.33) | copy-start | bytes 6291460
  1258.0 59.9 %copy-start.44 = (f32[1024]{0:T(1024)S(1)}, f32[1024]{0:T(1024)}, u32[]{:S(2)}) copy-start(f32[1024]{0:T(1024)} %get-tuple-element.365) | copy-start | bytes 12292
  1258.0 120.4 %all-gather.17.cloned.1.call-start = ((), (), s32[]{:S(2)}) async-start(), calls=%async_computation.13 | async-start | bytes 6291456 | tf_op jit(solution)/shard_map/all_gather | solution.py:265
  1312.5 5.5 copy-start.6
  1321.5 974.1 %reduce-scatter.14.cloned.1.call-start = ((), (), s32[]{:S(2)}) async-start(), calls=%async_computation.14 | async-start | bytes 6291456 | tf_op jit(solution)/shard_map/reduce_scatter | solution.py:292
  1386.6 10.6 copy-start.34
  1730.7 6.7 copy-start.14
  1730.7 6.7 copy-start.16
  1745.3 3.2 copy-start.54
  1748.4 5.9 copy-start.25
  1748.5 5.8 copy-start.27
  1748.5 5.8 copy-start.28
  1748.5 5.9 copy-start.30
  1764.3 533.8 %reduce-scatter.10.cloned.1.call-start = ((), (), s32[]{:S(2)}) async-start(), calls=%async_computation.10 | async-start | bytes 6291456 | tf_op jit(solution)/shard_map/reduce_scatter | solution.py:183
  2207.1 237.6 %reduce-scatter.20.cloned.1.call-start = ((), (), s32[]{:S(2)}) async-start(), calls=%async_computation.20 | async-start | bytes 17825792 | tf_op jit(solution)/shard_map/reduce_scatter | solution.py:243
  2231.3 395.5 %reduce-scatter.16.cloned.1.call-start = ((), (), s32[]{:S(2)}) async-start(), calls=%async_computation.16 | async-start | bytes 17825792 | tf_op jit(solution)/shard_map/reduce_scatter | solution.py:237
  2255.7 553.3 %reduce-scatter.18.cloned.1.call-start = ((), (), s32[]{:S(2)}) async-start(), calls=%async_computation.18 | async-start | bytes 17825792 | tf_op jit(solution)/shard_map/reduce_scatter | solution.py:240
  2280.3 7.7 copy-start.18
  2280.3 631.0 %all-reduce.4.cloned.1.call-start = ((), (), s32[]{:S(2)}) async-start(), calls=%async_computation.23 | async-start | bytes 4194304 | tf_op jit(solution)/shard_map/psum | solution.py:308
  2281.0 7.0 copy-start.22
  2288.0 4.2 copy-start.52
  2292.2 3.5 copy-start.11
  2292.2 3.5 copy-start.49
  2295.6 674.3 %all-gather.19.cloned.1.call-start = ((), (), s32[]{:S(2)}) async-start(), calls=%async_computation.15 | async-start | bytes 6291456 | tf_op jit(solution)/shard_map/all_gather | solution.py:303
  2305.4 794.2 %all-gather.27.cloned.1.call-start = ((), (), s32[]{:S(2)}) async-start(), calls=%async_computation.22 | async-start | bytes 17825792 | tf_op jit(solution)/shard_map/all_gather | solution.py:305
  2311.7 497.4 %copy-start.55 = (u32[32]{0:T(128)S(1)}, u32[32]{0:T(128)}, u32[]{:S(2)}) copy-start(u32[32]{0:T(128)} %constant.139) | copy-start | bytes 388
  2311.7 498.0 %copy-start.50 = (bf16[1024]{0:T(1024)(128)(2,1)S(1)}, bf16[1024]{0:T(1024)(128)(2,1)}, u32[]{:S(2)}) copy-start(bf16[1024]{0:T(1024)(128)(2,1)} %get-tuple-element.266) | copy-start | bytes 6148
  2311.7 498.0 %copy-start.51 = (bf16[1024]{0:T(1024)(128)(2,1)S(1)}, bf16[1024]{0:T(1024)(128)(2,1)}, u32[]{:S(2)}) copy-start(bf16[1024]{0:T(1024)(128)(2,1)} %get-tuple-element.349) | copy-start | bytes 6148
  2311.7 915.3 %all-gather.25.cloned.1.call-start = ((), (), s32[]{:S(2)}) async-start(), calls=%async_computation.21 | async-start | bytes 17825792 | tf_op jit(solution)/shard_map/all_gather | solution.py:254
  2444.7 909.5 %all-gather.21.cloned.1.call-start = ((), (), s32[]{:S(2)}) async-start(), calls=%async_computation.17 | async-start | bytes 17825792 | tf_op jit(solution)/shard_map/all_gather | solution.py:248
  2626.8 854.8 %all-gather.23.cloned.1.call-start = ((), (), s32[]{:S(2)}) async-start(), calls=%async_computation.19 | async-start | bytes 17825792 | tf_op jit(solution)/shard_map/all_gather | solution.py:251
  3509.1 4.7 copy-start.1
  (22 other events, 44.7 us)
Sparse Core Ops, SparseCore 0:
  9.6 59.4 all-gather.10
  211.2 99.2 reduce-scatter.7
  312.1 56.7 all-gather.14
  370.9 56.7 all-gather.12
  1258.1 54.3 reduce-scatter.11
  1321.7 56.7 all-gather.16
  1764.4 54.2 reduce-scatter.13
  2207.2 54.7 reduce-scatter.9
  2266.1 178.5 reduce-scatter.19
  2449.2 177.5 reduce-scatter.15
  2631.5 177.5 reduce-scatter.17
  2813.9 97.3 all-reduce.3
  2913.5 56.2 all-gather.18
  2972.7 126.8 all-gather.26
  3101.9 125.0 all-gather.24
  3229.2 124.9 all-gather.20
  3356.5 125.0 all-gather.22
